TPU v7x, 32 devices: a whole 2x2x4 slice. The times are simulated.
32 devices in a mesh: rows: 8 (over y, x, core), loop: 4 (over z).
Axes of the slice: x: 2, y: 2, z: 4, core: 2. Of those that a mesh axis runs over, the one named last changes fastest.
Arguments:
- integrals: float32 [2, 2, 8192, 8192], P(None, None, 'rows', 'loop'), may hold values from -6 to 6
- mask: int32 [2, 64, 64], P(None, 'rows', 'loop'), may hold values 0 or 1
- coeffs: float32 [8192, 640], P('loop'), may hold values from -0.0625 to 0.0625
Outputs:
- exchange: float32 [8192, 8192], P('rows', 'loop')
All inputs are finite; a program needn't handle non-finite values. No bound on the sum of `mask` on one device may be relied on, other than what follows from the above.
Results may differ from a plain program's by a relative error of at most 0.00009.
Values sent between devices are 32-bit elements; how exact they have to be, the bound alone decides.
A program may use at most 192 MiB of HBM per device.

v0:
```python
import jax
import jax.numpy as jnp
from jax import lax
from jax.sharding import PartitionSpec as P

TILE = 128


def local(integrals, mask, coeffs):
    nslab, naux, mrows, lcols = integrals.shape
    blocks = mask.astype(jnp.float32)[:, None, :, None, :, None]
    shaped = integrals.reshape(nslab, naux, mrows // TILE, TILE, lcols // TILE, TILE)
    masked = (shaped * blocks).reshape(nslab * naux, mrows, lcols)
    norbit = coeffs.shape[1]
    loops = lax.axis_size("loop")
    row_count = lax.axis_size("rows")
    mine = norbit // loops
    ratio = row_count // loops
    depth = norbit * nslab * naux
    row_full = lax.psum(
        jnp.einsum("pml,li->ipm", masked, coeffs, precision=lax.Precision.HIGHEST), "loop"
    )
    own_orbits = lax.dynamic_slice_in_dim(row_full, lax.axis_index("loop") * mine, mine, 0)
    row_flat = row_full.reshape(depth, mrows)
    sub_rows = mrows // row_count
    split_rows = own_orbits.reshape(mine, nslab * naux, row_count, sub_rows)
    routed = lax.all_to_all(
        lax.all_to_all(split_rows, "rows", split_axis=2, concat_axis=2, tiled=True),
        "loop",
        split_axis=2,
        concat_axis=0,
        tiled=True,
    )
    piece = lax.all_gather(routed, "rows", axis=3, tiled=True)
    flat = piece.reshape(depth, ratio, piece.shape[3])
    tiles = jnp.einsum("dm,doc->moc", row_flat, flat, precision=lax.Precision.HIGHEST)
    total = tiles.reshape(mrows, lcols)
    scale = 1.0 / jnp.sqrt(jnp.float32(depth))
    return total * scale


def solution(mesh):
    in_specs = (P(None, None, "rows", "loop"), P(None, "rows", "loop"), P("loop", None))
    out_specs = P("rows", "loop")
    return jax.shard_map(local, mesh=mesh, in_specs=in_specs, out_specs=out_specs, check_vma=False)
```

profile of v0, /device:TPU:0, one launch (start us, length us, event | category | flops | bytes accessed | tf_op | source)
XLA Modules:
  0.0 881.7 jit_solution(2462211604459332383)
XLA Ops:
  6.5 0.0 all-reduce.2.cloned.1.call-start
  6.5 0.7 convert_element_type.3
  7.2 11.0 %mul.20 = f32[2,2,8,128,16,128]{5,4,3,2,1,0:T(8,128)} broadcast(f32[2,8,16]{2,1,0:T(8,128)S(1)} %convert_element_type.3), dimensions={0,2,4} | broadcast | bytes 33555456 | tf_op jit(solution)/shard_map/mul | solution.py:13
  18.3 35.5 %mul.21 = f32[4,1024,2048]{2,1,0:T(8,128)} reshape(f32[2,2,8,128,16,128]{5,4,3,2,1,0:T(8,128)} %mul.20) | data formatting | bytes 67108864 | tf_op jit(solution)/shard_map/mul | solution.py:13
  53.7 32.9 %bitcast_multiply_fusion = f32[4,1024,2048]{2,1,0:T(8,128)} fusion(f32[4,1024,2048]{2,1,0:T(8,128)} %mul.21, f32[2,2,1024,2048]{3,2,1,0:T(8,128)} %param.3), kind=kLoop, calls=%fused_computation | loop fusion | flops 8388608 | bytes 100663296 | tf_op jit(solution)/shard_map/mul | solution.py:13
  86.6 87.8 %fusion.2 = f32[640,4,1024]{0,2,1:T(8,128)} fusion(f32[4,1024,2048]{2,1,0:T(8,128)} %bitcast_multiply_fusion, f32[2048,640]{1,0:T(8,128)} %param.5), kind=kOutput, calls=%fused_computation.4 | convolution fusion | flops 64424509440 | bytes 49283072 | tf_op jit(solution)/shard_map/pml,li->ipm/dot_general | solution.py:21
  174.4 0.0 all-reduce.2.cloned.1.call-update
  174.5 0.2 all-gather.2.cloned.1.call-start
  174.7 361.1 %all-reduce.2.cloned.1.call-done = f32[640,4,1024]{0,2,1:T(8,128)} async-done(((f32[640,4,1024]{0,2,1:T(8,128)}), f32[640,4,1024]{0,2,1:T(8,128)}) %all-reduce.2.cloned.1.call-update) | async-done | bytes 10485776 | tf_op jit(solution)/shard_map/psum | solution.py:20
  535.8 5.9 constant_dynamic-slice_fusion
  541.7 4.1 copy.15
  545.9 35.6 %all_to_all.23 = f32[160,4,8,128]{3,0,1,2:T(8,128)S(1)} all-to-all(f32[160,4,8,128]{3,0,1,2:T(8,128)S(1)} %copy.15), channel_id=1, replica_groups=mesh['rows'=8,'loop'=4] {'rows'}, dimensions={2} | all-to-all | bytes 5242880 | tf_op jit(solution)/shard_map/all_to_all | solution.py:28
  581.5 61.6 %all_to_all.24 = f32[160,4,8,128]{3,0,1,2:T(8,128)S(1)} all-to-all(f32[160,4,8,128]{3,0,1,2:T(8,128)S(1)} %all_to_all.23), channel_id=1, replica_groups=mesh['rows'=8,'loop'=4] {'loop'}, dimensions={2} | all-to-all | bytes 5242880 | tf_op jit(solution)/shard_map/all_to_all | solution.py:27
  643.1 1.7 copy.17
  644.8 0.0 all-gather.2.cloned.1.call-update
  644.8 13.2 %copy.13 = f32[640,4,1024]{2,1,0:T(4,128)} copy(f32[640,4,1024]{0,2,1:T(8,128)} %all-reduce.2.cloned.1.call-done) | data formatting | bytes 20971520 | tf_op jit(solution)/shard_map/psum | solution.py:20
  658.1 12.4 %reshape.19 = f32[2560,1024]{1,0:T(8,128)} reshape(f32[640,4,1024]{2,1,0:T(4,128)} %copy.13) | data formatting | bytes 20971520 | tf_op jit(solution)/shard_map/reshape | solution.py:24
  670.4 84.0 %all-gather.2.cloned.1.call-done = f32[640,4,2,1024]{3,0,2,1:T(8,128)} async-done(((f32[640,4,2,128]{3,0,2,1:T(8,128)}), f32[640,4,2,1024]{3,0,2,1:T(8,128)}) %all-gather.2.cloned.1.call-update) | async-done | bytes 20971536 | tf_op jit(solution)/shard_map/all_gather | solution.py:34
  754.4 34.2 %copy.18 = f32[640,4,2,1024]{3,2,1,0:T(2,128)S(1)} copy(f32[640,4,2,1024]{3,0,2,1:T(8,128)} %all-gather.2.cloned.1.call-done) | data formatting | bytes 41943040 | tf_op jit(solution)/shard_map/all_gather | solution.py:34
  788.6 13.6 %copy.22 = f32[320,8,2,1024]{3,1,2,0:T(8,128)} copy(f32[320,8,2,1024]{3,2,1,0:T(2,128)S(1)} %bitcast.26) | data formatting | bytes 41943040
  802.2 72.6 %convolution_multiply_fusion = f32[1024,2048]{1,0:T(8,128)} fusion(f32[2560,1024]{1,0:T(8,128)} %reshape.19, f32[2048,2560]{0,1:T(8,128)} %bitcast.27), kind=kOutput, calls=%fused_computation.3 | convolution fusion | flops 64426606592 | bytes 39845888 | tf_op jit(solution)/shard_map/dm,doc->moc/dot_general | solution.py:36
Async XLA Ops:
  6.5 529.3 %all-reduce.2.cloned.1.call-start = ((), (), s32[]{:S(2)}) async-start(), calls=%async_computation.2 | async-start | bytes 20971520 | tf_op jit(solution)/shard_map/psum | solution.py:20
  174.5 580.0 %all-gather.2.cloned.1.call-start = ((), (), s32[]{:S(2)}) async-start(), calls=%async_computation.3 | async-start | bytes 23592960 | tf_op jit(solution)/shard_map/all_gather | solution.py:34
Sparse Core Ops, SparseCore 0:
  174.6 361.1 all-reduce.1
  645.0 109.4 all-gather.1
where the time goes:
time: 883 us; the launch traced here: 882 us
  waiting for transfers between devices  445 us (50%)
  matrix products  160 us (18%)
  local copies, waits for them, and re-layouts  132 us (15%)
  blocking collectives  97.3 us (11%)
  other arithmetic  33.6 us (4%)
  between operations  13.4 us (2%)
    psum x1, waiting for transfers between devices, local(): lax.psum(jnp.einsum('pml,li->ipm', masked, coeffs, precision=lax.Precisio...  361 us
    dot_general x1, matrix products, local(): jnp.einsum('pml,li->ipm', masked, coeffs, precision=lax.Precision.HIGHEST)  87.8 us
    all_gather x1, waiting for transfers between devices, local(): piece = lax.all_gather(routed, 'rows', axis=3, tiled=True)  84 us
    dot_general x1, matrix products, local(): jnp.einsum('dm,doc->moc', row_flat, flat, precision=lax.Precision.HIGHEST)  72.6 us
    all_to_all x1, blocking collectives, local(): lax.all_to_all(lax.all_to_all(split_rows, 'rows', split_axis=2, concat_ax...  61.6 us
    mul x2, local copies, waits for them, and re-layouts, local(): masked = (shaped * blocks).reshape(nslab * naux, mrows, lcols)  46.5 us
    all_to_all x1, blocking collectives, local(): lax.all_to_all(split_rows, 'rows', split_axis=2, concat_axis=2, tiled=True)  35.6 us
    all_gather x1, local copies, waits for them, and re-layouts, local(): piece = lax.all_gather(routed, 'rows', axis=3, tiled=True)  34.2 us
  transfers between devices with their start and end apart: 2, of which 2 were waited for; matrix products, arithmetic and copies ran while one was open for 3% of the time, Pallas kernels for 0%

commit v1 on v0

--- a/solution.py
+++ b/solution.py
@@ -17,8 +17,11 @@
     mine = norbit // loops
     ratio = row_count // loops
     depth = norbit * nslab * naux
-    row_full = lax.psum(
-        jnp.einsum("pml,li->ipm", masked, coeffs, precision=lax.Precision.HIGHEST), "loop"
+    row_full = jnp.sum(
+        lax.all_gather(
+            jnp.einsum("pml,li->ipm", masked, coeffs, precision=lax.Precision.HIGHEST), "loop"
+        ),
+        axis=0,
     )
     own_orbits = lax.dynamic_slice_in_dim(row_full, lax.axis_index("loop") * mine, mine, 0)
     row_flat = row_full.reshape(depth, mrows)

time: 883 us -> 1310 us (1.48)
  waiting for transfers between devices: 445 us -> 786 us
  local copies, waits for them, and re-layouts: 132 us -> 180 us
  other arithmetic: 33.6 us -> 65.4 us
    all_gather x0 -> x1, waiting for transfers between devices: none -> 702 us  [local(): lax.all_gather(jnp.einsum('pml,li->ipm', masked, coeffs, precision=lax.Pr...]
    psum x1 -> x0, waiting for transfers between devices: 361 us -> none  [local(): lax.psum(jnp.einsum('pml,li->ipm', masked, coeffs, precision=lax.Precisio...]
    all_gather x0 -> x1, local copies, waits for them, and re-layouts: none -> 48.5 us  [local(): lax.all_gather(jnp.einsum('pml,li->ipm', masked, coeffs, precision=lax.Pr...]
    reduce_sum x0 -> x1, other arithmetic: none -> 31.8 us  [local(): jnp.sum(lax.all_gather(jnp.einsum('pml,li->ipm', masked, coeffs, precisio...]
    reduce_sum x0 -> x1, local copies, waits for them, and re-layouts: none -> 13.2 us  [local(): jnp.sum(lax.all_gather(jnp.einsum('pml,li->ipm', masked, coeffs, precisio...]
    psum x1 -> x0, local copies, waits for them, and re-layouts: 13.2 us -> none  [local(): lax.psum(jnp.einsum('pml,li->ipm', masked, coeffs, precision=lax.Precisio...]
  transfers between devices with their start and end apart: 2 -> 2, of which waited for: 2 -> 2; matrix products, arithmetic and copies ran while one was open for 3% -> 2% of each run, Pallas kernels for 0% -> 0%
where the time goes in v1:
time: 1310 us; the launch traced here: 1300 us
  waiting for transfers between devices  786 us (60%)
  local copies, waits for them, and re-layouts  180 us (14%)
  matrix products  161 us (12%)
  blocking collectives  97.3 us (7%)
  other arithmetic  65.4 us (5%)
  between operations  13.8 us (1%)
    all_gather x1, waiting for transfers between devices, local(): lax.all_gather(jnp.einsum('pml,li->ipm', masked, coeffs, precision=lax.Pr...  702 us
    dot_general x1, matrix products, local(): jnp.einsum('pml,li->ipm', masked, coeffs, precision=lax.Precision.HIGHEST)  87.8 us
    all_gather x1, waiting for transfers between devices, local(): piece = lax.all_gather(routed, 'rows', axis=3, tiled=True)  84 us
    dot_general x1, matrix products, local(): jnp.einsum('dm,doc->moc', row_flat, flat, precision=lax.Precision.HIGHEST)  72.8 us
    all_to_all x1, blocking collectives, local(): lax.all_to_all(lax.all_to_all(split_rows, 'rows', split_axis=2, concat_ax...  61.6 us
    all_gather x1, local copies, waits for them, and re-layouts, local(): lax.all_gather(jnp.einsum('pml,li->ipm', masked, coeffs, precision=lax.Pr...  48.5 us
    mul x2, local copies, waits for them, and re-layouts, local(): masked = (shaped * blocks).reshape(nslab * naux, mrows, lcols)  46.5 us
    all_to_all x1, blocking collectives, local(): lax.all_to_all(split_rows, 'rows', split_axis=2, concat_axis=2, tiled=True)  35.6 us
  transfers between devices with their start and end apart: 2, of which 2 were waited for; matrix products, arithmetic and copies ran while one was open for 2% of the time, Pallas kernels for 0%

profile of v1, /device:TPU:0, one launch (start us, length us, event | category | flops | bytes accessed | tf_op | source)
XLA Modules:
  0.0 1303.8 jit_solution(8994078772651873090)
XLA Ops:
  6.5 0.0 all-gather.6.cloned.1.call-start
  6.5 0.7 convert_element_type.3
  7.2 11.0 mul.20
  18.3 35.5 %mul.21 = f32[4,1024,2048]{2,1,0:T(8,128)} reshape(f32[2,2,8,128,16,128]{5,4,3,2,1,0:T(8,128)} %mul.20) | data formatting | bytes 67108864 | tf_op jit(solution)/shard_map/mul | solution.py:13
  53.7 32.9 %bitcast_multiply_fusion = f32[4,1024,2048]{2,1,0:T(8,128)} fusion(f32[4,1024,2048]{2,1,0:T(8,128)} %mul.21, f32[2,2,1024,2048]{3,2,1,0:T(8,128)} %param.3), kind=kLoop, calls=%fused_computation | loop fusion | flops 8388608 | bytes 100663296 | tf_op jit(solution)/shard_map/mul | solution.py:13
  86.6 87.8 %fusion.2 = f32[640,4,1024]{0,2,1:T(8,128)} fusion(f32[4,1024,2048]{2,1,0:T(8,128)} %bitcast_multiply_fusion, f32[2048,640]{1,0:T(8,128)} %param.5), kind=kOutput, calls=%fused_computation.4 | convolution fusion | flops 64424509440 | bytes 49283072 | tf_op jit(solution)/shard_map/pml,li->ipm/dot_general | solution.py:22
  174.4 0.0 all-gather.6.cloned.1.call-update
  174.5 0.2 all-gather.4.cloned.1.call-start
  174.7 702.4 %all-gather.6.cloned.1.call-done = f32[2560,4,1024]{0,2,1:T(8,128)} async-done(((f32[640,4,1024]{0,2,1:T(8,128)}), f32[2560,4,1024]{0,2,1:T(8,128)}) %all-gather.6.cloned.1.call-update) | async-done | bytes 41943056 | tf_op jit(solution)/shard_map/all_gather | solution.py:21
  877.1 48.5 %reshape.22 = f32[4,640,4,1024]{1,0,3,2:T(4,128)} reshape(f32[2560,4,1024]{0,2,1:T(8,128)} %all-gather.6.cloned.1.call-done) | data formatting | bytes 83886080 | tf_op jit(solution)/shard_map/all_gather | solution.py:21
  925.5 31.8 %reduce_sum.9 = f32[640,4,1024]{0,2,1:T(8,128)} reduce(f32[4,640,4,1024]{1,0,3,2:T(4,128)} %reshape.22, f32[]{:T(128)} %constant.6.clone.1), dimensions={0}, to_apply=%region_0.0 | reduce | flops 7864320 | bytes 52428804 | tf_op jit(solution)/shard_map/reduce_sum | solution.py:20
  957.3 5.9 constant_dynamic-slice_fusion
  963.3 4.1 copy.15
  967.4 35.6 %all_to_all.23 = f32[160,4,8,128]{3,0,1,2:T(8,128)S(1)} all-to-all(f32[160,4,8,128]{3,0,1,2:T(8,128)S(1)} %copy.15), channel_id=1, replica_groups=mesh['rows'=8,'loop'=4] {'rows'}, dimensions={2} | all-to-all | bytes 5242880 | tf_op jit(solution)/shard_map/all_to_all | solution.py:31
  1003.0 61.6 %all_to_all.24 = f32[160,4,8,128]{3,0,1,2:T(8,128)S(1)} all-to-all(f32[160,4,8,128]{3,0,1,2:T(8,128)S(1)} %all_to_all.23), channel_id=1, replica_groups=mesh['rows'=8,'loop'=4] {'loop'}, dimensions={2} | all-to-all | bytes 5242880 | tf_op jit(solution)/shard_map/all_to_all | solution.py:30
  1064.7 1.7 copy.17
  1066.4 0.0 all-gather.4.cloned.1.call-update
  1066.4 13.2 %copy.13 = f32[640,4,1024]{2,1,0:T(4,128)} copy(f32[640,4,1024]{0,2,1:T(8,128)} %reduce_sum.9) | data formatting | bytes 20971520 | tf_op jit(solution)/shard_map/reduce_sum | solution.py:20
  1079.6 12.4 reshape.19
  1092.0 84.0 %all-gather.4.cloned.1.call-done = f32[640,4,2,1024]{3,0,2,1:T(8,128)} async-done(((f32[640,4,2,128]{3,0,2,1:T(8,128)}), f32[640,4,2,1024]{3,0,2,1:T(8,128)}) %all-gather.4.cloned.1.call-update) | async-done | bytes 20971536 | tf_op jit(solution)/shard_map/all_gather | solution.py:37
  1176.0 34.2 %copy.18 = f32[640,4,2,1024]{3,2,1,0:T(2,128)S(1)} copy(f32[640,4,2,1024]{3,0,2,1:T(8,128)} %all-gather.4.cloned.1.call-done) | data formatting | bytes 41943040 | tf_op jit(solution)/shard_map/all_gather | solution.py:37
  1210.2 13.6 %copy.22 = f32[320,8,2,1024]{3,1,2,0:T(8,128)} copy(f32[320,8,2,1024]{3,2,1,0:T(2,128)S(1)} %bitcast.28) | data formatting | bytes 41943040
  1223.8 72.8 %convolution_multiply_fusion = f32[1024,2048]{1,0:T(8,128)} fusion(f32[2560,1024]{1,0:T(8,128)} %reshape.19, f32[2048,2560]{0,1:T(8,128)} %bitcast.29), kind=kOutput, calls=%fused_computation.3 | convolution fusion | flops 64426606592 | bytes 39845888 | tf_op jit(solution)/shard_map/dm,doc->moc/dot_general | solution.py:39
Async XLA Ops:
  6.5 870.5 %all-gather.6.cloned.1.call-start = ((), (), s32[]{:S(2)}) async-start(), calls=%async_computation.3 | async-start | bytes 52428800 | tf_op jit(solution)/shard_map/all_gather | solution.py:21
  174.5 1001.5 %all-gather.4.cloned.1.call-start = ((), (), s32[]{:S(2)}) async-start(), calls=%async_computation.2 | async-start | bytes 23592960 | tf_op jit(solution)/shard_map/all_gather | solution.py:37
Sparse Core Ops, SparseCore 0:
  174.6 702.4 all-gather.5
  1066.5 109.4 all-gather.3
